TPU v7x, 512 devices: a whole 4x8x8 slice. The times are simulated.
512 devices in a mesh: ctx: 64 (over y, x, core), tp: 8 (over z).
Axes of the slice: x: 4, y: 8, z: 8, core: 2. Of those that a mesh axis runs over, the one named last changes fastest.
Arguments:
- queries: bfloat16 [16384, 8192], P('ctx', 'tp'), may hold values from -6 to 6
- key_branch: bfloat16 [16384, 8192], P('ctx', 'tp'), may hold values from -6 to 6
- value_branch: bfloat16 [16384, 8192], P('ctx', 'tp'), may hold values from -6 to 6
- cotangent: bfloat16 [16384, 8192], P('ctx', 'tp'), may hold values from -6 to 6
- filters: float32 [512, 128], replicated, may hold values from -0.5 to 0.5
- skip_bias: float32 [8192], P('tp'), may hold values from -1 to 1
- contig_start: int32 [16384], replicated, may hold values from 0 to 16383, as said below
Outputs:
- output: bfloat16 [16384, 8192], P('ctx', 'tp')
- grad_query: bfloat16 [16384, 8192], P('ctx', 'tp')
- grad_key: bfloat16 [16384, 8192], P('ctx', 'tp')
- grad_value: bfloat16 [16384, 8192], P('ctx', 'tp')
- grad_filter: float32 [512, 128], replicated
- grad_bias: float32 [8192], P('tp')
Inputs may be any that keep to these rules, and one draw needn't show every extreme that they name: contig_start[0] is 0, and for t > 0 contig_start[t] is either t (a new contig begins) or contig_start[t - 1]; the last token begins a contig of its own.
All inputs are finite; a program needn't handle non-finite values.
Results may differ from a plain program's by a relative error of at most 0.0056.
Values may be sent and summed in bfloat16 or wider, within the bound.
A program may use at most 64 MiB of HBM per device.

v0:
```python
import math

import jax
import jax.numpy as jnp
from jax import lax
from jax.sharding import PartitionSpec as P


def toeplitz(filter_taps):
    group_count, filter_size = filter_taps.shape
    leading = jnp.zeros((group_count, 1), filter_taps.dtype)
    trailing = jnp.zeros((group_count, filter_size), filter_taps.dtype)
    pattern = jnp.concatenate([leading, filter_taps[:, ::-1], trailing], axis=1)
    tiled = jnp.tile(pattern, (1, filter_size))[:, : 2 * filter_size * filter_size]
    return tiled.reshape(group_count, filter_size, 2 * filter_size)


def fold_lags(products):
    group_count, filter_size, window_size = products.shape
    flattened = products.reshape(group_count, filter_size * window_size)
    flattened = jnp.concatenate(
        [flattened, jnp.zeros((group_count, filter_size), products.dtype)], axis=1
    )
    columns = flattened.reshape(group_count, filter_size, window_size + 1).sum(axis=1)
    return columns[:, 1 : filter_size + 1][:, ::-1]


def hyena_pass(
    queries,
    key_branch,
    value_branch,
    cotangent,
    gated_signal,
    signal_grad,
    left_rim,
    right_rim,
    row_starts,
    next_starts,
    filter_taps,
    bias_part,
    first_row,
):
    row_count, channel_count = gated_signal.shape
    group_count, filter_size = filter_taps.shape
    per_group = channel_count // group_count
    block_count = row_count // filter_size
    padded = jnp.concatenate(
        [jnp.zeros((1, channel_count), jnp.bfloat16), left_rim, gated_signal], axis=0
    )
    windows = jnp.concatenate(
        [
            padded[:row_count].reshape(block_count, filter_size, group_count, per_group),
            padded[filter_size:].reshape(block_count, filter_size, group_count, per_group),
        ],
        axis=1,
    )
    grads_ext = jnp.concatenate(
        [signal_grad, right_rim, jnp.zeros((1, channel_count), jnp.bfloat16)], axis=0
    )
    grads_ext = grads_ext.reshape(block_count + 1, filter_size, group_count, per_group)
    starts_ext = jnp.concatenate([row_starts, next_starts]).reshape(block_count + 1, filter_size)
    source_pos = (
        first_row + (jnp.arange(block_count + 1, dtype=jnp.int32)[:, None] - 1) * filter_size
    )
    source_pos = source_pos + jnp.arange(2 * filter_size, dtype=jnp.int32)[None, :]
    visible = source_pos[:, None, :] >= starts_ext[:, :, None]
    band = jnp.where(visible[:, None], toeplitz(filter_taps)[None], jnp.zeros((), jnp.bfloat16))
    convolved = jnp.einsum(
        "bgts,bsgc->btgc", band[:block_count], windows, preferred_element_type=jnp.float32
    ).reshape(row_count, channel_count)
    back_terms = jnp.einsum("bgts,btgc->bsgc", band, grads_ext, preferred_element_type=jnp.float32)
    gated_grad = (back_terms[:block_count, filter_size:] + back_terms[1:, :filter_size]).reshape(
        row_count, channel_count
    )
    filtered = convolved + bias_part[None, :] * gated_signal.astype(jnp.float32)
    output = (queries.astype(jnp.float32) * filtered).astype(jnp.bfloat16)
    grad_query = (cotangent.astype(jnp.float32) * filtered).astype(jnp.bfloat16)
    gated_grad = gated_grad + bias_part[None, :] * signal_grad.astype(jnp.float32)
    grad_key = (gated_grad * value_branch.astype(jnp.float32)).astype(jnp.bfloat16)
    grad_value = (gated_grad * key_branch.astype(jnp.float32)).astype(jnp.bfloat16)
    bias_term = jnp.sum(signal_grad.astype(jnp.float32) * gated_signal.astype(jnp.float32), axis=0)
    products = jnp.einsum(
        "btgc,bsgc->bgts", grads_ext[:block_count], windows, preferred_element_type=jnp.float32
    )
    products = jnp.where(visible[:block_count, None], products, jnp.zeros((), jnp.float32)).sum(
        axis=0
    )
    return (output, grad_query, grad_key, grad_value, fold_lags(products), bias_term)


def gate_pair(first_input, second_input):
    return (first_input.astype(jnp.float32) * second_input.astype(jnp.float32)).astype(jnp.bfloat16)


def body(queries, key_branch, value_branch, cotangent, filters, skip_bias, contig_start):
    row_count, channel_count = queries.shape
    group_total, filter_size = filters.shape
    ctx_count = lax.axis_size("ctx")
    tp_count = lax.axis_size("tp")
    shard_index = lax.axis_index("ctx")
    tensor_index = lax.axis_index("tp")
    token_count = row_count * ctx_count
    per_group = channel_count * tp_count // group_total
    starts_pad = jnp.concatenate([contig_start, jnp.zeros((filter_size,), jnp.int32)])
    moved = (
        lax.all_to_all(queries, "ctx", split_axis=1, concat_axis=0, tiled=True),
        lax.all_to_all(key_branch, "ctx", split_axis=1, concat_axis=0, tiled=True),
        lax.all_to_all(value_branch, "ctx", split_axis=1, concat_axis=0, tiled=True),
        lax.all_to_all(cotangent, "ctx", split_axis=1, concat_axis=0, tiled=True),
    )
    query_full, key_full, value_full, cotangent_full = moved
    column_count = channel_count // ctx_count
    held_groups = max(1, column_count // per_group)
    gated_signal = gate_pair(key_full, value_full)
    signal_grad = gate_pair(cotangent_full, query_full)
    group_first = (tensor_index * channel_count + shard_index * column_count) // per_group
    filter_taps = lax.dynamic_slice_in_dim(filters, group_first, held_groups, 0).astype(
        jnp.bfloat16
    )
    bias_slice = lax.dynamic_slice_in_dim(skip_bias, shard_index * column_count, column_count, 0)
    slab_rows = 8 * filter_size
    slab_count = token_count // slab_rows
    signal_pad = jnp.concatenate(
        [jnp.zeros((filter_size - 1, column_count), jnp.bfloat16), gated_signal], axis=0
    )
    grad_pad = jnp.concatenate(
        [signal_grad, jnp.zeros((filter_size - 1, column_count), jnp.bfloat16)], axis=0
    )

    def one_slab(slab_index):
        first_row = slab_index * slab_rows

        def rows_of(array):
            return lax.dynamic_slice_in_dim(array, first_row, slab_rows, 0)

        return hyena_pass(
            rows_of(query_full),
            rows_of(key_full),
            rows_of(value_full),
            rows_of(cotangent_full),
            rows_of(gated_signal),
            rows_of(signal_grad),
            lax.dynamic_slice_in_dim(signal_pad, first_row, filter_size - 1, 0),
            lax.dynamic_slice_in_dim(grad_pad, first_row + slab_rows, filter_size - 1, 0),
            lax.dynamic_slice_in_dim(contig_start, first_row, slab_rows, 0),
            lax.dynamic_slice_in_dim(starts_pad, first_row + slab_rows, filter_size, 0),
            filter_taps,
            bias_slice,
            first_row,
        )

    pieces = lax.map(one_slab, jnp.arange(slab_count, dtype=jnp.int32))
    results = tuple((piece.reshape(token_count, column_count) for piece in pieces[:4]))
    returned = (
        lax.all_to_all(results[0], "ctx", split_axis=0, concat_axis=1, tiled=True),
        lax.all_to_all(results[1], "ctx", split_axis=0, concat_axis=1, tiled=True),
        lax.all_to_all(results[2], "ctx", split_axis=0, concat_axis=1, tiled=True),
        lax.all_to_all(results[3], "ctx", split_axis=0, concat_axis=1, tiled=True),
    )
    output, grad_query, grad_key, grad_value = returned
    filter_part = lax.dynamic_update_slice(
        jnp.zeros((group_total, filter_size), jnp.float32), pieces[4].sum(axis=0), (group_first, 0)
    )
    bias_part = lax.dynamic_update_slice(
        jnp.zeros((channel_count,), jnp.float32),
        pieces[5].sum(axis=0),
        (shard_index * column_count,),
    )
    filter_sum = lax.psum(filter_part, ("ctx", "tp"))
    bias_sum = lax.psum(bias_part, "ctx")
    grad_filter = filter_sum * (1.0 / math.sqrt(token_count * per_group))
    grad_bias = bias_sum * (1.0 / math.sqrt(token_count))
    return (output, grad_query, grad_key, grad_value, grad_filter, grad_bias)


def solution(mesh):
    return jax.shard_map(
        body,
        mesh=mesh,
        in_specs=(
            P("ctx", "tp"),
            P("ctx", "tp"),
            P("ctx", "tp"),
            P("ctx", "tp"),
            P(),
            P("tp"),
            P(),
        ),
        out_specs=(P("ctx", "tp"), P("ctx", "tp"), P("ctx", "tp"), P("ctx", "tp"), P(), P("tp")),
        check_vma=False,
    )
```

profile of v0, /device:TPU:1, one launch (start us, length us, event | category | flops | bytes accessed | tf_op | source)
XLA Modules:
  0.0 609.1 jit_solution(8776793197152598005)
XLA Ops:
  7.2 2.1 copy.73
  9.3 11.7 %all-to-all-start.1 = ((bf16[256,64,16]{0,2,1:T(8,128)(2,1)}), bf16[256,64,16]{0,2,1:T(8,128)(2,1)S(1)}, u32[]{:S(2)}, u32[]{:S(2)}) async-start(bf16[256,64,16]{0,2,1:T(8,128)(2,1)} %bitcast.17), calls=%async_computation.1 | async-start | bytes 1048576 | tf_op jit(solution)/shard_map/all_to_all | solution.py:107
  21.0 1.0 copy.75
  22.0 16.7 %all-to-all-done.1 = bf16[256,64,16]{0,2,1:T(8,128)(2,1)S(1)} async-done(((bf16[256,64,16]{0,2,1:T(8,128)(2,1)}), bf16[256,64,16]{0,2,1:T(8,128)(2,1)S(1)}, u32[]{:S(2)}, u32[]{:S(2)}) %all-to-all-start.1) | async-done | bytes 524320 | tf_op jit(solution)/shard_map/all_to_all | solution.py:107
  38.7 5.7 all-to-all-start.2
  45.4 16.7 %all-to-all-done.2 = bf16[256,64,16]{0,2,1:T(8,128)(2,1)S(1)} async-done(((bf16[256,64,16]{0,2,1:T(8,128)(2,1)}), bf16[256,64,16]{0,2,1:T(8,128)(2,1)S(1)}, u32[]{:S(2)}, u32[]{:S(2)}) %all-to-all-start.2) | async-done | bytes 524320 | tf_op jit(solution)/shard_map/all_to_all | solution.py:108
  62.1 5.7 all-to-all-start
  68.8 16.7 %all-to-all-done = bf16[256,64,16]{0,2,1:T(8,128)(2,1)S(1)} async-done(((bf16[256,64,16]{0,2,1:T(8,128)(2,1)}), bf16[256,64,16]{0,2,1:T(8,128)(2,1)S(1)}, u32[]{:S(2)}, u32[]{:S(2)}) %all-to-all-start) | async-done | bytes 524320 | tf_op jit(solution)/shard_map/all_to_all | solution.py:106
  85.5 5.8 all-to-all-start.3
  92.3 16.7 %all-to-all-done.3 = bf16[256,64,16]{0,2,1:T(8,128)(2,1)S(1)} async-done(((bf16[256,64,16]{0,2,1:T(8,128)(2,1)}), bf16[256,64,16]{0,2,1:T(8,128)(2,1)S(1)}, u32[]{:S(2)}, u32[]{:S(2)}) %all-to-all-start.3) | async-done | bytes 524320 | tf_op jit(solution)/shard_map/all_to_all | solution.py:109
  109.2 1.0 concatenate.42
  111.1 1.9 concatenate.44
  113.0 122.1 %while.22 = (s32[]{:T(128)}, bf16[16,1024,16]{1,2,0:T(8,128)(2,1)}, bf16[16,1024,16]{1,2,0:T(8,128)(2,1)}, bf16[16,1024,16]{1,2,0:T(8,128)(2,1)}, bf16[16,1024,1...) while((s32[]{:T(128)}, bf16[16,1024,16]{1,2,0:T(8,128)(2,1)}, ...), condition=%wide.region_4.5_spmd, body=%wide.region_0.4_spmd.sunk | while | flops 28791580 | bytes 4254939 | solution.py:152
  235.1 1.3 copy.79
  236.8 1.1 copy.80
  237.8 5.8 all-to-all-start.4
  244.3 1.1 copy.82
  245.4 16.0 %all-to-all-done.4 = bf16[64,256,16]{1,2,0:T(8,128)(2,1)S(1)} async-done(((bf16[64,256,16]{1,2,0:T(8,128)(2,1)}), bf16[64,256,16]{1,2,0:T(8,128)(2,1)S(1)}, u32[]{:S(2)}, u32[]{:S(2)}) %all-to-all-start.4) | async-done | bytes 524320 | tf_op jit(solution)/shard_map/all_to_all | solution.py:155
  261.4 5.9 all-to-all-start.5
  267.9 1.1 copy.84
  269.0 16.0 %all-to-all-done.5 = bf16[64,256,16]{1,2,0:T(8,128)(2,1)S(1)} async-done(((bf16[64,256,16]{1,2,0:T(8,128)(2,1)}), bf16[64,256,16]{1,2,0:T(8,128)(2,1)S(1)}, u32[]{:S(2)}, u32[]{:S(2)}) %all-to-all-start.5) | async-done | bytes 524320 | tf_op jit(solution)/shard_map/all_to_all | solution.py:156
  284.9 5.7 all-to-all-start.6
  291.3 1.1 copy.86
  292.4 16.0 %all-to-all-done.6 = bf16[64,256,16]{1,2,0:T(8,128)(2,1)S(1)} async-done(((bf16[64,256,16]{1,2,0:T(8,128)(2,1)}), bf16[64,256,16]{1,2,0:T(8,128)(2,1)S(1)}, u32[]{:S(2)}, u32[]{:S(2)}) %all-to-all-start.6) | async-done | bytes 524320 | tf_op jit(solution)/shard_map/all_to_all | solution.py:157
  308.3 5.7 all-to-all-start.7
  315.2 129.0 %psum.15 = f32[1024]{0:T(1024)S(1)} all-reduce(f32[1024]{0:T(1024)S(1)} %dynamic_update_slice.46), channel_id=1, replica_groups=mesh['ctx'=64,'tp'=8] {'ctx'}, use_global_device_ids=true, to_apply=%region_8.9 | all-reduce | flops 1024 | bytes 8192 | tf_op jit(solution)/shard_map/psum | solution.py:170
  444.8 151.8 %all-reduce.6.cloned.1.call-done = f32[512,128]{1,0:T(8,128)} async-done(((f32[512,128]{1,0:T(8,128)}), f32[512,128]{1,0:T(8,128)}) %all-reduce.6.cloned.1.call-update) | async-done | bytes 262160 | tf_op jit(solution)/shard_map/psum | solution.py:169
  596.6 1.7 broadcast_multiply_fusion
  598.2 1.0 copy.87
  599.2 1.0 copy.88
  600.2 1.0 copy.89
  601.2 1.0 copy.90
  (741 shorter events, 117.3 us)
Async XLA Ops:
  7.2 85.0 %copy-start = (f32[512,128]{1,0:T(8,128)S(1)}, f32[512,128]{1,0:T(8,128)}, u32[]{:S(2)}) copy-start(f32[512,128]{1,0:T(8,128)} %param.13) | copy-start | bytes 786436
  9.3 11.8 %copy-start.2 = (bf16[256,1024]{1,0:T(8,128)(2,1)S(1)}, bf16[256,1024]{1,0:T(8,128)(2,1)}, u32[]{:S(2)}) copy-start(bf16[256,1024]{1,0:T(8,128)(2,1)} %param.11) | copy-start | bytes 1572868
  9.3 29.4 %all-to-all-start.1 = ((bf16[256,64,16]{0,2,1:T(8,128)(2,1)}), bf16[256,64,16]{0,2,1:T(8,128)(2,1)S(1)}, u32[]{:S(2)}, u32[]{:S(2)}) async-start(bf16[256,64,16]{0,2,1:T(8,128)(2,1)} %bitcast.17), calls=%async_computation.1 | async-start | bytes 1048576 | tf_op jit(solution)/shard_map/all_to_all | solution.py:107
  22.0 22.4 %copy-start.3 = (bf16[256,1024]{1,0:T(8,128)(2,1)S(1)}, bf16[256,1024]{1,0:T(8,128)(2,1)}, u32[]{:S(2)}) copy-start(bf16[256,1024]{1,0:T(8,128)(2,1)} %param.9) | copy-start | bytes 1572868
  38.7 23.4 %all-to-all-start.2 = ((bf16[256,64,16]{0,2,1:T(8,128)(2,1)}), bf16[256,64,16]{0,2,1:T(8,128)(2,1)S(1)}, u32[]{:S(2)}, u32[]{:S(2)}) async-start(bf16[256,64,16]{0,2,1:T(8,128)(2,1)} %bitcast.19), calls=%async_computation.2 | async-start | bytes 1048576 | tf_op jit(solution)/shard_map/all_to_all | solution.py:108
  45.4 22.4 %copy-start.4 = (bf16[256,1024]{1,0:T(8,128)(2,1)S(1)}, bf16[256,1024]{1,0:T(8,128)(2,1)}, u32[]{:S(2)}) copy-start(bf16[256,1024]{1,0:T(8,128)(2,1)} %param.12) | copy-start | bytes 1572868
  62.1 23.4 %all-to-all-start = ((bf16[256,64,16]{0,2,1:T(8,128)(2,1)}), bf16[256,64,16]{0,2,1:T(8,128)(2,1)S(1)}, u32[]{:S(2)}, u32[]{:S(2)}) async-start(bf16[256,64,16]{0,2,1:T(8,128)(2,1)} %bitcast.15), calls=%async_computation | async-start | bytes 1048576 | tf_op jit(solution)/shard_map/all_to_all | solution.py:106
  85.5 5.9 copy-start.8
  85.5 23.5 %all-to-all-start.3 = ((bf16[256,64,16]{0,2,1:T(8,128)(2,1)}), bf16[256,64,16]{0,2,1:T(8,128)(2,1)S(1)}, u32[]{:S(2)}, u32[]{:S(2)}) async-start(bf16[256,64,16]{0,2,1:T(8,128)(2,1)} %bitcast.21), calls=%async_computation.3 | async-start | bytes 1048576 | tf_op jit(solution)/shard_map/all_to_all | solution.py:109
  237.8 5.8 copy-start.5
  237.8 23.5 %all-to-all-start.4 = ((bf16[64,256,16]{1,2,0:T(8,128)(2,1)}), bf16[64,256,16]{1,2,0:T(8,128)(2,1)S(1)}, u32[]{:S(2)}, u32[]{:S(2)}) async-start(bf16[64,256,16]{1,2,0:T(8,128)(2,1)} %copy.80), calls=%async_computation.4 | async-start | bytes 1048576 | tf_op jit(solution)/shard_map/all_to_all | solution.py:155
  245.4 21.8 %copy-start.6 = (bf16[16,1024,16]{1,2,0:T(8,128)(2,1)S(1)}, bf16[16,1024,16]{1,2,0:T(8,128)(2,1)}, u32[]{:S(2)}) copy-start(bf16[16,1024,16]{1,2,0:T(8,128)(2,1)} %get-tuple-element.260) | copy-start | bytes 1572868
  261.4 23.6 %all-to-all-start.5 = ((bf16[64,256,16]{1,2,0:T(8,128)(2,1)}), bf16[64,256,16]{1,2,0:T(8,128)(2,1)S(1)}, u32[]{:S(2)}, u32[]{:S(2)}) async-start(bf16[64,256,16]{1,2,0:T(8,128)(2,1)} %copy.82), calls=%async_computation.5 | async-start | bytes 1048576 | tf_op jit(solution)/shard_map/all_to_all | solution.py:156
  269.0 21.7 %copy-start.7 = (bf16[16,1024,16]{1,2,0:T(8,128)(2,1)S(1)}, bf16[16,1024,16]{1,2,0:T(8,128)(2,1)}, u32[]{:S(2)}) copy-start(bf16[16,1024,16]{1,2,0:T(8,128)(2,1)} %get-tuple-element.261) | copy-start | bytes 1572868
  284.9 23.4 %all-to-all-start.6 = ((bf16[64,256,16]{1,2,0:T(8,128)(2,1)}), bf16[64,256,16]{1,2,0:T(8,128)(2,1)S(1)}, u32[]{:S(2)}, u32[]{:S(2)}) async-start(bf16[64,256,16]{1,2,0:T(8,128)(2,1)} %copy.84), calls=%async_computation.6 | async-start | bytes 1048576 | tf_op jit(solution)/shard_map/all_to_all | solution.py:157
  308.3 292.9 %all-to-all-start.7 = ((bf16[64,256,16]{1,2,0:T(8,128)(2,1)}), bf16[64,256,16]{1,2,0:T(8,128)(2,1)S(1)}, u32[]{:S(2)}, u32[]{:S(2)}) async-start(bf16[64,256,16]{1,2,0:T(8,128)(2,1)} %copy.86), calls=%async_computation.7 | async-start | bytes 1048576 | tf_op jit(solution)/shard_map/all_to_all | solution.py:158
  314.0 282.5 %all-reduce.6.cloned.1.call-start = ((), (), s32[]{:S(2)}) async-start(), calls=%async_computation.8 | async-start | bytes 524288 | tf_op jit(solution)/shard_map/psum | solution.py:169
  314.2 0.7 copy-start.1
Sparse Core Ops, SparseCore 0:
  320.4 276.1 all-reduce.5
where the time goes:
time: 612 us; the launch traced here: 609 us
  waiting for transfers between devices  266 us (43%)
  blocking collectives  129 us (21%)
  local copies, waits for them, and re-layouts  81.4 us (13%)
  starting transfers between devices  52.1 us (9%)
  other arithmetic  36.6 us (6%)
  matrix products  16.5 us (3%)
  between operations  14.4 us (2%)
  loops' own time  12.7 us (2%)
    psum x1, waiting for transfers between devices, body(): filter_sum = lax.psum(filter_part, ('ctx', 'tp'))  152 us
    psum x1, blocking collectives, body(): bias_sum = lax.psum(bias_part, 'ctx')  129 us
    all_to_all x1, waiting for transfers between devices, body(): lax.all_to_all(queries, 'ctx', split_axis=1, concat_axis=0, tiled=True)  16.7 us
    all_to_all x1, waiting for transfers between devices, body(): lax.all_to_all(key_branch, 'ctx', split_axis=1, concat_axis=0, tiled=True)  16.7 us
    all_to_all x1, waiting for transfers between devices, body(): lax.all_to_all(value_branch, 'ctx', split_axis=1, concat_axis=0, tiled=True)  16.7 us
    all_to_all x1, waiting for transfers between devices, body(): lax.all_to_all(cotangent, 'ctx', split_axis=1, concat_axis=0, tiled=True)  16.7 us
    all_to_all x1, waiting for transfers between devices, body(): lax.all_to_all(results[2], 'ctx', split_axis=0, concat_axis=1, tiled=True)  16 us
    all_to_all x1, waiting for transfers between devices, body(): lax.all_to_all(results[0], 'ctx', split_axis=0, concat_axis=1, tiled=True)  16 us
  transfers between devices with their start and end apart: 9, of which 8 were waited for; matrix products, arithmetic and copies ran while one was open for 2% of the time, Pallas kernels for 0%

commit v1 on v0

v1 whole, which is shorter than its diff:
```python
import functools
import math

import jax
import jax.numpy as jnp
from jax import lax
from jax.experimental import pallas as pl
from jax.experimental.pallas import tpu as pltpu
from jax.sharding import PartitionSpec as P

F32 = jnp.float32
BF16 = jnp.bfloat16
MESH = pl.DeviceIdType.MESH
ROW = 8
NT = (((1,), (1,)), ((), ()))


def iotas():
    down = lax.broadcasted_iota(jnp.int32, (128, 128), 0)
    across = lax.broadcasted_iota(jnp.int32, (128, 128), 1)
    return down, across


def conv_kernel(
    starts_ref, q_ref, k_ref, v_ref, c_ref, uh_ref, gh_ref, f_ref, b_ref,
    o_ref, gq_ref, gk_ref, gv_ref, gf_ref, gb_ref, pair_ref, lag_ref, ct_ref, bt_ref,
):
    s, t = iotas()

    @pl.when(pl.program_id(0) == 0)
    def _():
        start = [jnp.broadcast_to(starts_ref[i : i + 1, :], (128, 128)) for i in range(3)]
        lower = (s <= t).astype(F32)
        for b in range(3):
            pair_ref[2 * b] = ((1.0 - lower) * (s + 128 * (b - 1) >= start[b]).astype(F32)).astype(BF16)
            if b < 2:
                pair_ref[2 * b + 1] = (lower * (s + 128 * b >= start[b]).astype(F32)).astype(BF16)
                limit = jnp.where(127 - s <= t, start[b], start[b + 1])
                lag_ref[b] = (127 - s + 128 * b >= limit).astype(F32)

    q, k, v, c = (ref[...].astype(F32) for ref in (q_ref, k_ref, v_ref, c_ref))
    u = (k * v).astype(BF16)
    g = (c * q).astype(BF16)
    u_turned = jnp.concatenate([uh_ref[...], u], axis=0).T
    g_turned = jnp.concatenate([g, gh_ref[...]], axis=0).T
    gb_ref[...] = jnp.sum(u.astype(F32) * g.astype(F32), axis=0, keepdims=True)
    taps = f_ref[...].astype(BF16).astype(F32)
    flip = (s + t == 127).astype(F32).astype(BF16)
    flipped = [
        jnp.dot(flip, u[128 * i : 128 * i + 128], preferred_element_type=F32).astype(BF16)
        for i in range(2)
    ]
    upper = 127 - s <= t
    owner = lax.shift_right_logical(t, 4)
    none = jnp.zeros((128, 128), BF16)
    for i in range(8):
        rows = slice(16 * i, 16 * i + 16)
        ring = pltpu.roll(
            jnp.broadcast_to(taps[i : i + 1, :], (128, 128)), 0, 1, stride=1, stride_axis=0
        ).astype(BF16)
        p0, c0, p1, c1, p2 = (ring * pair_ref[n] for n in range(5))
        u_rows, g_rows = u_turned[rows], g_turned[rows]
        ct_ref[rows, 0:128] = jnp.dot(
            u_rows[:, 0:256], jnp.concatenate([p0, c0], 0), preferred_element_type=F32
        )
        ct_ref[rows, 128:256] = jnp.dot(
            u_rows[:, 128:384], jnp.concatenate([p1, c1], 0), preferred_element_type=F32
        )
        bt_ref[rows, 0:128] = lax.dot_general(
            g_rows[:, 0:256], jnp.concatenate([c0, p1], 1), NT, preferred_element_type=F32
        )
        bt_ref[rows, 128:256] = lax.dot_general(
            g_rows[:, 128:384], jnp.concatenate([c1, p2], 1), NT, preferred_element_type=F32
        )
        mine = owner == i
        first = jnp.dot(
            jnp.where(mine, flipped[0], none), g_turned[:, 0:256], preferred_element_type=F32
        )
        second = jnp.dot(
            jnp.where(mine, flipped[1], none), g_turned[:, 128:384], preferred_element_type=F32
        )
        lags = jnp.where(upper, first[:, :128], first[:, 128:]) * lag_ref[0]
        lags = lags + jnp.where(upper, second[:, :128], second[:, 128:]) * lag_ref[1]
        lags = pltpu.roll(lags, 1, 1, stride=1, stride_axis=0)
        gf_ref[i : i + 1, :] = jnp.sum(lags, axis=0, keepdims=True)
    bias = b_ref[...]
    filtered = ct_ref[...].T + bias * u.astype(F32)
    o_ref[...] = (q * filtered).astype(BF16)
    gq_ref[...] = (c * filtered).astype(BF16)
    gated_grad = bt_ref[...].T + bias * g.astype(F32)
    gk_ref[...] = (gated_grad * v).astype(BF16)
    gv_ref[...] = (gated_grad * k).astype(BF16)


def conv(starts, q, k, v, c, u_halo, g_halo, taps, bias):
    tokens, channels = q.shape
    tile = pl.BlockSpec((tokens, 128), lambda i: (0, i))
    halo = pl.BlockSpec((128, 128), lambda i: (0, i))
    line = pl.BlockSpec((1, 128), lambda i: (0, i))
    group = pl.BlockSpec((8, 128), lambda i: (i, 0))
    return pl.pallas_call(
        conv_kernel,
        grid=(channels // 128,),
        in_specs=[pl.BlockSpec((8, 128), lambda i: (0, 0))] + [tile] * 4 + [halo] * 2 + [group, line],
        out_specs=[tile] * 4 + [group, line],
        out_shape=[jax.ShapeDtypeStruct((tokens, channels), BF16)] * 4
        + [
            jax.ShapeDtypeStruct((channels // 16, 128), F32),
            jax.ShapeDtypeStruct((1, channels), F32),
        ],
        scratch_shapes=[
            pltpu.VMEM((5, 128, 128), BF16),
            pltpu.VMEM((2, 128, 128), F32),
            pltpu.VMEM((128, 256), F32),
            pltpu.VMEM((128, 256), F32),
        ],
    )(starts, q, k, v, c, u_halo, g_halo, taps, bias)


def reduce_kernel(
    part_ref, bias_ref, out_ref, bias_out_ref, row_in, col_in, bias_row, bias_col, total,
    row_s, row_r, col_s, col_r, brow_s, brow_r, bcol_s, bcol_r, z_s, z_r, x_s, x_r, c_s, c_r, out_sem,
):
    shard = lax.axis_index("ctx")
    z = lax.axis_index("tp")
    columns = lax.axis_size("ctx") // ROW
    layers = lax.axis_size("tp")
    place = lax.rem(shard, ROW)
    y = shard // ROW
    x, core = place // 2, lax.rem(place, 2)

    def along_row(step):
        to = lax.rem(place + step, ROW)
        return to, {"ctx": y * ROW + to, "tp": z}

    def along_y(step):
        to = lax.rem(y + step, columns)
        return to, {"ctx": to * ROW + place, "tp": z}

    def along_z(step):
        to = lax.rem(z + step, layers)
        return to, {"ctx": shard, "tp": to}

    def along_x(step):
        to = lax.rem(x + step, ROW // 2)
        return to, {"ctx": y * ROW + to * 2 + core, "tp": z}

    other = {"ctx": y * ROW + x * 2 + 1 - core, "tp": z}
    routes = [(along_row, ROW), (along_y, columns), (along_z, layers)]

    barrier = pltpu.get_barrier_semaphore()
    for route, size in routes:
        for step in range(1, size):
            pl.semaphore_signal(barrier, inc=1, device_id=route(step)[1], device_id_type=MESH)
    pl.semaphore_wait(barrier, sum(size - 1 for _, size in routes))

    def copy(source, target, send, receive, device):
        return pltpu.make_async_remote_copy(
            src_ref=source, dst_ref=target, send_sem=send, recv_sem=receive,
            device_id=device, device_id_type=MESH,
        )

    sent = []

    def send(*args):
        descriptor = copy(*args)
        descriptor.start()
        sent.append(descriptor)

    for step in range(1, ROW):
        to, device = along_row(step)
        send(part_ref.at[to], row_in.at[place], row_s.at[step], row_r.at[place], device)
        send(bias_ref, bias_row.at[place], brow_s.at[step], brow_r.at[place], device)
    row_in[place] = part_ref[place]
    bias_row[place] = bias_ref[...]
    for step in range(1, ROW):
        source, device = along_row(step)
        copy(part_ref.at[0], row_in.at[source], row_s.at[step], row_r.at[source], device).wait_recv()
        copy(bias_ref, bias_row.at[source], brow_s.at[step], brow_r.at[source], device).wait_recv()
    col_in[y] = jnp.sum(row_in[...], axis=0)
    bias_col[y] = jnp.sum(bias_row[...], axis=0)
    for step in range(1, columns):
        _, device = along_y(step)
        send(col_in.at[y], col_in.at[y], col_s.at[step], col_r.at[y], device)
        send(bias_col.at[y], bias_col.at[y], bcol_s.at[step], bcol_r.at[y], device)
    for step in range(1, columns):
        source, device = along_y(step)
        copy(col_in.at[y], col_in.at[source], col_s.at[step], col_r.at[source], device).wait_recv()
        copy(bias_col.at[y], bias_col.at[source], bcol_s.at[step], bcol_r.at[source], device).wait_recv()
    total[z, place] = jnp.sum(col_in[...], axis=0)
    bias_out_ref[...] = jnp.sum(bias_col[...], axis=0)
    for step in range(1, layers):
        _, device = along_z(step)
        send(total.at[z, place], total.at[z, place], z_s.at[step], z_r.at[z], device)
    for step in range(1, layers):
        source, device = along_z(step)
        copy(total.at[z, place], total.at[source, place], z_s.at[step], z_r.at[source], device).wait_recv()
    for step in range(1, ROW // 2):
        _, device = along_x(step)
        send(total.at[:, place], total.at[:, place], x_s.at[step], x_r.at[x], device)
    send(total.at[:, place], total.at[:, place], c_s.at[0], c_r.at[x], other)
    for step in range(1, ROW // 2):
        source, device = along_x(step)
        block = total.at[:, source * 2 + core]
        copy(block, block, x_s.at[step], x_r.at[source], device).wait_recv()
        send(block, block, c_s.at[step], c_r.at[source], other)
    for source in range(ROW // 2):
        block = total.at[:, source * 2 + 1 - core]
        copy(block, block, c_s.at[0], c_r.at[source], other).wait_recv()
    done = pltpu.make_async_copy(total, out_ref, out_sem)
    done.start()
    for descriptor in sent:
        descriptor.wait_send()
    done.wait()


def reduce(columns, layers, part, bias):
    dma = pltpu.SemaphoreType.DMA
    slice_shape = part.shape[1:]
    return pl.pallas_call(
        reduce_kernel,
        in_specs=[pl.BlockSpec(memory_space=pltpu.VMEM)] * 2,
        out_specs=[pl.BlockSpec(memory_space=pl.ANY), pl.BlockSpec(memory_space=pltpu.VMEM)],
        out_shape=[
            jax.ShapeDtypeStruct((layers, ROW, *slice_shape), F32),
            jax.ShapeDtypeStruct(bias.shape, F32),
        ],
        scratch_shapes=[
            pltpu.VMEM((ROW, *slice_shape), F32),
            pltpu.VMEM((columns, *slice_shape), F32),
            pltpu.VMEM((ROW, *bias.shape), F32),
            pltpu.VMEM((columns, *bias.shape), F32),
            pltpu.VMEM((layers, ROW, *slice_shape), F32),
            dma((ROW,)), dma((ROW,)), dma((columns,)), dma((columns,)),
            dma((ROW,)), dma((ROW,)), dma((columns,)), dma((columns,)),
            dma((layers,)), dma((layers,)), dma((ROW // 2,)), dma((ROW // 2,)),
            dma((ROW // 2,)), dma((ROW // 2,)), dma,
        ],
        compiler_params=pltpu.CompilerParams(collective_id=0, has_side_effects=True),
    )(part, bias)


def body(q, k, v, c, filters, bias, contig_start):
    tokens, channels = q.shape
    group_total, taps = filters.shape
    count, layers = lax.axis_size("ctx"), lax.axis_size("tp")
    shard, z = lax.axis_index("ctx"), lax.axis_index("tp")
    groups = group_total // layers
    token_count = tokens * count

    def gate(a, b):
        return (a.astype(F32) * b.astype(F32)).astype(BF16)

    u_edge = gate(k[-taps:], v[-taps:])
    g_edge = gate(c[:taps], q[:taps])
    u_halo = lax.ppermute(u_edge, "ctx", [(i, (i + 1) % count) for i in range(count)])
    g_halo = lax.ppermute(g_edge, "ctx", [(i, (i - 1) % count) for i in range(count)])
    far = jnp.full((6 * taps,), token_count, jnp.int32)
    starts = lax.dynamic_slice_in_dim(jnp.concatenate([contig_start, far]), shard * tokens, 8 * taps)
    starts = starts.reshape(8, taps) - shard * tokens
    mine = lax.dynamic_slice_in_dim(filters, z * groups, groups, 0)
    o, gq, gk, gv, part, bias_part = conv(
        starts, q, k, v, c, u_halo, g_halo, mine, bias.reshape(1, channels)
    )
    total, bias_total = reduce(
        count // ROW, layers, part.reshape(ROW, groups // ROW, taps), bias_part.reshape(8, channels // 8)
    )
    grad_filter = total.reshape(group_total, taps) * (1.0 / math.sqrt(token_count * (channels // groups)))
    grad_bias = bias_total.reshape(channels) * (1.0 / math.sqrt(token_count))
    return o, gq, gk, gv, grad_filter, grad_bias


def solution(mesh):
    return jax.shard_map(
        body,
        mesh=mesh,
        in_specs=(P("ctx", "tp"),) * 4 + (P(), P("tp"), P()),
        out_specs=(P("ctx", "tp"),) * 4 + (P(), P("tp")),
        check_vma=False,
    )
```

time: 612 us -> 65.8 us (0.11)
  waiting for transfers between devices: 266 us -> 0.21 us
  blocking collectives: 129 us -> 0 us
  local copies, waits for them, and re-layouts: 81.4 us -> 1.33 us
  Pallas kernels: 0 us -> 47.3 us
  starting transfers between devices: 52.1 us -> 10.7 us
  other arithmetic: 36.6 us -> 5.16 us
  matrix products: 16.5 us -> 0 us
  between operations: 14.4 us -> 0.73 us
  loops' own time: 12.7 us -> 0 us
    psum x1 -> x0, waiting for transfers between devices: 152 us -> none  [body(): filter_sum = lax.psum(filter_part, ('ctx', 'tp'))]
    psum x1 -> x0, blocking collectives: 129 us -> none  [body(): bias_sum = lax.psum(bias_part, 'ctx')]
    all_to_all x8 -> x0, waiting for transfers between devices: 115 us -> none  [the longest x1 16.7 us: body(): lax.all_to_all(queries, 'ctx', split_axis=1, concat_axis=0, tiled=True)]
    all_to_all x8 -> x0, starting transfers between devices: 52 us -> none  [the longest x1 11.7 us: body(): lax.all_to_all(key_branch, 'ctx', split_axis=1, concat_axis=0, tiled=True)]
    pallas_call x0 -> x2, Pallas kernels: none -> 47.3 us  [the longest x1 36.4 us: reduce(): pl.pallas_call(reduce_kernel, in_specs=[pl.BlockSpec(memory_space=pltpu.V...]
    dynamic_slice x65 -> x1, local copies, waits for them, and re-layouts: 24.2 us -> 0.6 us  [body(): mine = lax.dynamic_slice_in_dim(filters, z * groups, groups, 0)]
    dot_general x48 -> x0, matrix products: 16.5 us -> none  [the longest x16 5.89 us: hyena_pass(): jnp.einsum('btgc,bsgc->bgts', grads_ext[:block_count], windows, preferred...]
    reduce_sum x34 -> x0, other arithmetic: 14.7 us -> none  [the longest x16 14.1 us: hyena_pass(): jnp.sum(signal_grad.astype(jnp.float32) * gated_signal.astype(jnp.float32...]
  transfers between devices with their start and end apart: 9 -> 2, of which waited for: 8 -> 1; matrix products, arithmetic and copies ran while one was open for 2% -> 4% of each run, Pallas kernels for 0% -> 0%
where the time goes in v1:
time: 65.8 us; the launch traced here: 65.4 us
  Pallas kernels  47.3 us (72%)
  starting transfers between devices  10.7 us (16%)
  other arithmetic  5.16 us (8%)
  local copies, waits for them, and re-layouts  1.33 us (2%)
  between operations  0.73 us (1%)
    pallas_call x1, Pallas kernels, reduce(): pl.pallas_call(reduce_kernel, in_specs=[pl.BlockSpec(memory_space=pltpu.V...  36.4 us
    pallas_call x1, Pallas kernels, conv(): pl.pallas_call(conv_kernel, grid=(channels // 128,), in_specs=[pl.BlockSp...  10.9 us
    ppermute x1, starting transfers between devices, body(): lax.ppermute(g_edge, 'ctx', [(i, (i - 1) % count) for i in range(count)])  6.17 us
    ppermute x1, starting transfers between devices, body(): lax.ppermute(u_edge, 'ctx', [(i, (i + 1) % count) for i in range(count)])  4.5 us
    convert_element_type x2, other arithmetic, gate(): return (a.astype(F32) * b.astype(F32)).astype(BF16)  2.22 us
    mul x1, other arithmetic, body(): total.reshape(group_total, taps)  1.67 us
  transfers between devices with their start and end apart: 2, of which 1 were waited for; matrix products, arithmetic and copies ran while one was open for 4% of the time, Pallas kernels for 0%

profile of v1, /device:TPU:1, one launch (start us, length us, event | category | flops | bytes accessed | tf_op | source)
XLA Modules:
  0.0 65.4 jit_solution(3567499028798059577)
XLA Ops:
  0.6 0.0 copy-start
  0.6 0.0 copy-start.1
  0.7 1.2 %multiply_convert_fusion.1 = bf16[128,1024]{1,0:T(8,128)(2,1)S(1)} fusion(bf16[256,1024]{1,0:T(8,128)(2,1)} %v_ref.1, bf16[256,1024]{1,0:T(8,128)(2,1)} %k_ref.1), kind=kLoop, calls=%fused_computation.1 | loop fusion | flops 524288 | bytes 786432 | tf_op jit(solution)/shard_map/convert_element_type | solution.py:252
  1.8 4.5 %collective-permute-start = (bf16[128,1024]{1,0:T(8,128)(2,1)S(1)}, bf16[128,1024]{1,0:T(8,128)(2,1)S(1)}, u32[]{:S(2)}, u32[]{:S(2)}) collective-permute-start(bf16[128,1024]{1,0:T(8,128)(2,1)S(1)} %multiply_convert_fusion.1), channel_id=1, source_target_pairs={{0,8},{8,16},{16,24},{24,32},{32,40},{40,48},{48,56},{56,64},{64,7... | collective-permute-start | bytes 786440 | tf_op jit(solution)/shard_map/ppermute | solution.py:256
  6.3 0.0 copy-done.1
  6.3 0.0 copy-start.4
  6.4 1.1 %multiply_convert_fusion = bf16[128,1024]{1,0:T(8,128)(2,1)S(1)} fusion(bf16[256,1024]{1,0:T(8,128)(2,1)S(1)} %copy-done.1, bf16[256,1024]{1,0:T(8,128)(2,1)} %c_ref.1), kind=kLoop, calls=%fused_computation | loop fusion | flops 524288 | bytes 786432 | tf_op jit(solution)/shard_map/convert_element_type | solution.py:252
  7.4 6.2 %collective-permute-start.1 = (bf16[128,1024]{1,0:T(8,128)(2,1)S(1)}, bf16[128,1024]{1,0:T(8,128)(2,1)S(1)}, u32[]{:S(2)}, u32[]{:S(2)}) collective-permute-start(bf16[128,1024]{1,0:T(8,128)(2,1)S(1)} %multiply_convert_fusion), channel_id=1, source_target_pairs={{0,504},{8,0},{16,8},{24,16},{32,24},{40,32},{48,40},{56,48},{64,5... | collective-permute-start | bytes 786440 | tf_op jit(solution)/shard_map/ppermute | solution.py:257
  13.6 0.0 copy-done.4
  13.6 0.7 %subtract_bitcast_fusion.starts_ref = s32[8,128]{1,0:T(8,128)} fusion(s32[]{:T(128)S(6)} %select_n.6, s32[16384]{0:T(1024)S(1)} %copy-done.4, s32[]{:T(128)S(6)} %mul.31), kind=kLoop, calls=%fused_computation.5 | loop fusion | flops 1024 | bytes 69640 | tf_op jit(solution)/shard_map/sub | solution.py:260
  14.3 0.0 copy-done
  14.3 0.6 constant_dynamic-slice_fusion.f_ref
  14.9 0.0 collective-permute-done.uh_ref
  14.9 0.0 copy-start.2
  14.9 0.2 collective-permute-done.1.gh_ref
  15.1 0.0 copy-start.3
  15.1 0.5 copy-done.2
  15.6 0.2 copy-done.3
  15.8 10.9 %shard_map.118 = (bf16[256,1024]{1,0:T(8,128)(2,1)}, bf16[256,1024]{1,0:T(8,128)(2,1)}, bf16[256,1024]{1,0:T(8,128)(2,1)}, bf16[256,1024]{1,0:T(8,128)(2,1)}, f32[64,128]{1,0:T(8,128)}, /*index=5*/f32[1,1024]{1,0:T(1,128)}) custom-call(s32[8,128]{1,0:T(8,128)} %subtract_bitcast_fusion.starts_ref, bf16[256,1024]{1,0:T(8,128)(2,1)} %q_ref.1, ...), custom_call_target="tpu_custom_call" | custom-call | tf_op jit(solution)/shard_map/pallas_call | solution.py:101
  26.7 36.4 %shard_map.119 = (f32[8,8,8,128]{3,2,1,0:T(8,128)}, f32[8,128]{1,0:T(8,128)}) custom-call(f32[8,8,128]{2,1,0:T(8,128)} %bitcast.9, f32[8,128]{1,0:T(8,128)} %bitcast.11), custom_call_target="tpu_custom_call" | custom-call | tf_op jit(solution)/shard_map/pallas_call | solution.py:220
  63.1 0.0 copy-start.5
  63.1 1.7 %broadcast_multiply_fusion = f32[8,8,8,128]{3,2,1,0:T(8,128)} fusion(f32[8,8,8,128]{3,2,1,0:T(8,128)} %get-tuple-element.20), kind=kLoop, calls=%fused_computation.2 | loop fusion | flops 65536 | bytes 524288 | tf_op jit(solution)/shard_map/mul | solution.py:268
  64.8 0.0 copy-done.5
  64.8 0.6 multiply_bitcast_fusion
Async XLA Ops:
  0.6 13.7 %copy-start = (f32[512,128]{1,0:T(8,128)S(1)}, f32[512,128]{1,0:T(8,128)}, u32[]{:S(2)}) copy-start(f32[512,128]{1,0:T(8,128)} %param.11) | copy-start | bytes 786436
  0.6 5.7 %copy-start.1 = (bf16[256,1024]{1,0:T(8,128)(2,1)S(1)}, bf16[256,1024]{1,0:T(8,128)(2,1)}, u32[]{:S(2)}) copy-start(bf16[256,1024]{1,0:T(8,128)(2,1)} %q_ref.1) | copy-start | bytes 1572868
  1.8 13.1 %collective-permute-start = (bf16[128,1024]{1,0:T(8,128)(2,1)S(1)}, bf16[128,1024]{1,0:T(8,128)(2,1)S(1)}, u32[]{:S(2)}, u32[]{:S(2)}) collective-permute-start(bf16[128,1024]{1,0:T(8,128)(2,1)S(1)} %multiply_convert_fusion.1), channel_id=1, source_target_pairs={{0,8},{8,16},{16,24},{24,32},{32,40},{40,48},{48,56},{56,64},{64,7... | collective-permute-start | bytes 786440 | tf_op jit(solution)/shard_map/ppermute | solution.py:256
  6.3 7.3 %copy-start.4 = (s32[16384]{0:T(1024)S(1)}, s32[16384]{0:T(1024)}, u32[]{:S(2)}) copy-start(s32[16384]{0:T(1024)} %param.13) | copy-start | bytes 196612
  7.4 7.7 %collective-permute-start.1 = (bf16[128,1024]{1,0:T(8,128)(2,1)S(1)}, bf16[128,1024]{1,0:T(8,128)(2,1)S(1)}, u32[]{:S(2)}, u32[]{:S(2)}) collective-permute-start(bf16[128,1024]{1,0:T(8,128)(2,1)S(1)} %multiply_convert_fusion), channel_id=1, source_target_pairs={{0,504},{8,0},{16,8},{24,16},{32,24},{40,32},{48,40},{56,48},{64,5... | collective-permute-start | bytes 786440 | tf_op jit(solution)/shard_map/ppermute | solution.py:257
  14.9 0.7 %copy-start.2 = (bf16[128,1024]{1,0:T(8,128)(2,1)}, bf16[128,1024]{1,0:T(8,128)(2,1)S(1)}, u32[]{:S(2)}) copy-start(bf16[128,1024]{1,0:T(8,128)(2,1)S(1)} %collective-permute-done.uh_ref) | copy-start | bytes 786436
  15.1 0.7 %copy-start.3 = (bf16[128,1024]{1,0:T(8,128)(2,1)}, bf16[128,1024]{1,0:T(8,128)(2,1)S(1)}, u32[]{:S(2)}) copy-start(bf16[128,1024]{1,0:T(8,128)(2,1)S(1)} %collective-permute-done.1.gh_ref) | copy-start | bytes 786436
  63.1 1.7 %copy-start.5 = (f32[8,128]{1,0:T(8,128)S(1)}, f32[8,128]{1,0:T(8,128)}, u32[]{:S(2)}) copy-start(f32[8,128]{1,0:T(8,128)} %get-tuple-element.21) | copy-start | bytes 12292

commit v2 on v0

v2 whole, which is shorter than its diff:
```python
import functools
import math

import jax
import jax.numpy as jnp
from jax import lax
from jax.experimental import pallas as pl
from jax.experimental.pallas import tpu as pltpu
from jax.sharding import PartitionSpec as P

F32 = jnp.float32
BF16 = jnp.bfloat16
MESH = pl.DeviceIdType.MESH
XS = 4
NT = (((1,), (1,)), ((), ()))


def iotas():
    down = lax.broadcasted_iota(jnp.int32, (128, 128), 0)
    across = lax.broadcasted_iota(jnp.int32, (128, 128), 1)
    return down, across


def dot(a, b):
    return jnp.dot(a, b, preferred_element_type=F32)


def whole_kernel(
    filter_scale, bias_scale,
    q_hbm, k_hbm, v_hbm, c_hbm, filters_hbm, skip_hbm, starts_hbm,
    o_ref, gq_ref, gk_ref, gv_ref, total, bias_total,
    q_ref, k_ref, v_ref, c_ref, taps_ref, skip_ref, starts_ref,
    u_edge, g_edge, u_halo, g_halo, u_turned, g_turned, u_flip,
    pair_ref, lag_ref, ct_ref, bt_ref,
    part, half_in, x_in, y_in, bias_part, bias_x, bias_y,
    in_sem, misc_sem, us, ur, gs, gr,
    c_s, c_r, x_s, x_r, y_s, y_r, bc_s, bc_r, bx_s, bx_r, by_s, by_r,
    z_s, z_r, gx_s, gx_r, gc_s, gc_r,
):
    shard, z = lax.axis_index("ctx"), lax.axis_index("tp")
    count, layers = lax.axis_size("ctx"), lax.axis_size("tp")
    columns = count // (2 * XS)
    tiles = q_ref.shape[0]
    groups = part.shape[0] * part.shape[1] * part.shape[2]
    y, x, core = shard // (2 * XS), lax.rem(shard, 2 * XS) // 2, lax.rem(shard, 2)

    def device(to_y, to_x, to_core, to_z):
        return {"ctx": (to_y * XS + to_x) * 2 + to_core, "tp": to_z}

    def along_x(step):
        to = lax.rem(x + step, XS)
        return to, device(y, to, core, z)

    def along_y(step):
        to = lax.rem(y + step, columns)
        return to, device(to, x, core, z)

    def along_z(step):
        to = lax.rem(z + step, layers)
        return to, device(y, x, core, to)

    other = device(y, x, 1 - core, z)
    right = {"ctx": lax.rem(shard + 1, count), "tp": z}
    left = {"ctx": lax.rem(shard + count - 1, count), "tp": z}

    def inputs(i):
        lanes = pl.ds(pl.multiple_of(i * 128, 128), 128)
        return [
            pltpu.make_async_copy(hbm.at[:, lanes], ref.at[i], in_sem.at[n, i])
            for n, (hbm, ref) in enumerate(
                ((q_hbm, q_ref), (k_hbm, k_ref), (v_hbm, v_ref), (c_hbm, c_ref))
            )
        ]

    small = [
        pltpu.make_async_copy(starts_hbm, starts_ref, misc_sem.at[0]),
        pltpu.make_async_copy(filters_hbm.at[pl.ds(pl.multiple_of(z * groups, 8), groups)], taps_ref, misc_sem.at[1]),
        pltpu.make_async_copy(skip_hbm, skip_ref, misc_sem.at[2]),
    ]

    barrier = pltpu.get_barrier_semaphore()
    friends = [left, right, other] + [along_x(step)[1] for step in range(1, XS)]
    friends += [along_y(step)[1] for step in range(1, columns)]
    friends += [along_z(step)[1] for step in range(1, layers)]
    for friend in friends:
        pl.semaphore_signal(barrier, inc=1, device_id=friend, device_id_type=MESH)

    @pl.loop(0, tiles)
    def _(i):
        for copy in inputs(i):
            copy.start()

    for copy in small:
        copy.start()

    s, t = iotas()
    flip = (s + t == 127).astype(F32).astype(BF16)

    def gates(i):
        q, k, v, c = (ref[i].astype(F32) for ref in (q_ref, k_ref, v_ref, c_ref))
        return q, k, v, c, (k * v).astype(BF16), (c * q).astype(BF16)

    @pl.loop(0, tiles)
    def _(i):
        for copy in inputs(i):
            copy.wait()
        u_edge[i] = (k_ref[i, 128:256].astype(F32) * v_ref[i, 128:256].astype(F32)).astype(BF16)
        g_edge[i] = (c_ref[i, 0:128].astype(F32) * q_ref[i, 0:128].astype(F32)).astype(BF16)

    pl.semaphore_wait(barrier, len(friends))
    sent = []

    def remote(source, target, send, receive, to):
        return pltpu.make_async_remote_copy(
            src_ref=source, dst_ref=target, send_sem=send, recv_sem=receive,
            device_id=to, device_id_type=MESH,
        )

    def u_copy(i):
        return remote(u_edge.at[i], u_halo.at[i], us.at[i], ur.at[i], right)

    def g_copy(i):
        return remote(g_edge.at[i], g_halo.at[i], gs.at[i], gr.at[i], left)

    def send(*args):
        descriptor = remote(*args)
        descriptor.start()
        sent.append(descriptor)

    @pl.loop(0, tiles)
    def _(i):
        g_copy(i).start()

    @pl.loop(0, tiles)
    def _(i):
        u_copy(i).start()

    @pl.loop(0, tiles, unroll=2)
    def _(i):
        q, k, v, c, u, g = gates(i)
        u_turned[i, :, 128:384] = u.T
        g_turned[i, :, 0:256] = g.T
        u_flip[i, 0:128] = dot(flip, u[0:128]).astype(BF16)
        u_flip[i, 128:256] = dot(flip, u[128:256]).astype(BF16)
        bias_part[pl.ds(i, 1)] = jnp.sum(u.astype(F32) * g.astype(F32), axis=0, keepdims=True)

    for copy in small:
        copy.wait()
    first_row = shard * 256
    rows = [starts_ref[pl.ds(jnp.minimum(2 * shard + b, 2 * count - 1), 1), :] - first_row for b in range(3)]
    rows[2] = rows[2] + jnp.where(shard == count - 1, 256 * count, 0)
    start = [jnp.broadcast_to(row, (128, 128)) for row in rows]
    lower = (s <= t).astype(F32)
    turned = 127 - s
    upper = (turned <= t).astype(F32)
    for b in range(3):
        pair_ref[2 * b] = ((1.0 - lower) * (s + 128 * (b - 1) >= start[b]).astype(F32)).astype(BF16)
        if b < 2:
            pair_ref[2 * b + 1] = (lower * (s + 128 * b >= start[b]).astype(F32)).astype(BF16)
            lag_ref[2 * b] = upper * (turned + 128 * b >= start[b]).astype(F32)
            lag_ref[2 * b + 1] = (1.0 - upper) * (turned + 128 * b >= start[b + 1]).astype(F32)

    owner = lax.shift_right_logical(t, 4)
    none = jnp.zeros((128, 128), BF16)
    above = turned <= t

    def fold(lags):
        lags = pltpu.roll(lags, 1, 1, stride=1, stride_axis=0)
        return jnp.sum(lags, axis=0, keepdims=True)

    def part_rows(i):
        return part.at[i // XS, lax.rem(i, XS)]

    def own_lags(i):
        mine_part = part_rows(i)
        for n in range(8):
            mine = owner == n
            first = dot(jnp.where(mine, u_flip[i, 0:128], none), g_turned[i, :, 0:256])
            second = dot(jnp.where(mine, u_flip[i, 128:256], none), g_turned[i, :, 128:256])
            lags = jnp.where(above, first[:, :128] , first[:, 128:]) * (lag_ref[0] + lag_ref[1])
            mine_part[n : n + 1, :] = fold(lags + second * lag_ref[2])

    def halo_lags(i):
        mine_part = part_rows(i)
        g_turned[i, :, 256:384] = g_halo[i].T
        for n in range(8):
            mine = owner == n
            far = dot(jnp.where(mine, u_flip[i, 128:256], none), g_turned[i, :, 256:384])
            mine_part[n : n + 1, :] += fold(far * lag_ref[3])

    send(bias_part, bias_x.at[0], bc_s, bc_r, other)

    @pl.loop(0, tiles, unroll=2)
    def _(i):
        own_lags(i)

    remote(bias_part, bias_x.at[0], bc_s, bc_r, other).wait_recv()
    bias_x[1 + x] = bias_part[...] + bias_x[0]
    for step in range(1, XS):
        _, to = along_x(step)
        send(bias_x.at[1 + x], bias_x.at[1 + x], bx_s.at[step], bx_r.at[x], to)

    @pl.loop(0, tiles, unroll=2)
    def _(i):
        g_copy(i).wait_recv()
        halo_lags(i)

    send(part.at[1 - core], half_in, c_s, c_r, other)

    @pl.loop(0, tiles)
    def _(i):
        u_copy(i).wait_recv()
        u_turned[i, :, 0:128] = u_halo[i].T

    for step in range(1, XS):
        source, to = along_x(step)
        remote(bias_x.at[1 + x], bias_x.at[1 + source], bx_s.at[step], bx_r.at[source], to).wait_recv()
    bias_y[y] = bias_x[1] + bias_x[2] + bias_x[3] + bias_x[4]
    for step in range(1, columns):
        _, to = along_y(step)
        send(bias_y.at[y], bias_y.at[y], by_s.at[step], by_r.at[y], to)

    def conv(i):
        q, k, v, c, u, g = gates(i)
        taps = taps_ref[pl.ds(pl.multiple_of(i * 8, 8), 8)].astype(BF16).astype(F32)
        for n in range(8):
            span = slice(16 * n, 16 * n + 16)
            ring = pltpu.roll(
                jnp.broadcast_to(taps[n : n + 1, :], (128, 128)), 0, 1, stride=1, stride_axis=0
            ).astype(BF16)
            p0, c0, p1, c1, p2 = (ring * pair_ref[m] for m in range(5))
            u_rows, g_rows = u_turned[i, span], g_turned[i, span]
            ct_ref[span, 0:128] = dot(u_rows[:, 0:256], jnp.concatenate([p0, c0], 0))
            ct_ref[span, 128:256] = dot(u_rows[:, 128:384], jnp.concatenate([p1, c1], 0))
            bt_ref[span, 0:128] = lax.dot_general(
                g_rows[:, 0:256], jnp.concatenate([c0, p1], 1), NT, preferred_element_type=F32
            )
            bt_ref[span, 128:256] = lax.dot_general(
                g_rows[:, 128:384], jnp.concatenate([c1, p2], 1), NT, preferred_element_type=F32
            )
        skip = skip_ref[pl.ds(i, 1)]
        filtered = ct_ref[...].T + skip * u.astype(F32)
        lanes = pl.ds(pl.multiple_of(i * 128, 128), 128)
        o_ref[:, lanes] = (q * filtered).astype(BF16)
        gq_ref[:, lanes] = (c * filtered).astype(BF16)
        gated_grad = bt_ref[...].T + skip * g.astype(F32)
        gk_ref[:, lanes] = (gated_grad * v).astype(BF16)
        gv_ref[:, lanes] = (gated_grad * k).astype(BF16)

    remote(part.at[1 - core], half_in, c_s, c_r, other).wait_recv()
    part[core] += half_in[...]
    for step in range(1, XS):
        to_x, to = along_x(step)
        send(part.at[core, to_x], x_in.at[x], x_s.at[step], x_r.at[x], to)
    x_in[x] = part[core, x]

    pl.loop(0, tiles // 2, unroll=2)(conv)

    for step in range(1, XS):
        source, to = along_x(step)
        remote(x_in.at[x], x_in.at[source], x_s.at[step], x_r.at[source], to).wait_recv()
    y_in[y] = x_in[0] + x_in[1] + x_in[2] + x_in[3]
    for step in range(1, columns):
        _, to = along_y(step)
        send(y_in.at[y], y_in.at[y], y_s.at[step], y_r.at[y], to)

    pl.loop(tiles // 2, tiles, unroll=2)(conv)

    for step in range(1, columns):
        source, to = along_y(step)
        remote(y_in.at[y], y_in.at[source], y_s.at[step], y_r.at[source], to).wait_recv()
    total[z, core, x] = jnp.sum(y_in[...], axis=0) * filter_scale
    for step in range(1, layers):
        _, to = along_z(step)
        send(total.at[z, core, x], total.at[z, core, x], z_s.at[step], z_r.at[z], to)

    for step in range(1, columns):
        source, to = along_y(step)
        remote(bias_y.at[y], bias_y.at[source], by_s.at[step], by_r.at[source], to).wait_recv()
    bias_total[...] = jnp.sum(bias_y[...], axis=0) * bias_scale

    for step in range(1, layers):
        source, to = along_z(step)
        remote(total.at[z, core, x], total.at[source, core, x], z_s.at[step], z_r.at[source], to).wait_recv()
    block = total.at[:, core, x]
    for step in range(1, XS):
        _, to = along_x(step)
        send(block, block, gx_s.at[step], gx_r.at[x], to)
    send(block, block, gc_s.at[x], gc_r.at[x], other)
    for step in range(1, XS):
        source, to = along_x(step)
        block = total.at[:, core, source]
        remote(block, block, gx_s.at[step], gx_r.at[source], to).wait_recv()
        send(block, block, gc_s.at[source], gc_r.at[source], other)

    @pl.loop(0, tiles)
    def _(i):
        u_copy(i).wait_send()
        g_copy(i).wait_send()

    for source in range(XS):
        block = total.at[:, 1 - core, source]
        remote(block, block, gc_s.at[source], gc_r.at[source], other).wait_recv()
    for descriptor in sent:
        descriptor.wait_send()


def whole(columns, layers, scales, q, k, v, c, filters, skip, starts):
    tokens, channels = q.shape
    tiles = channels // 128
    slice_shape = (channels // 16 // (2 * XS), 128)
    dma = pltpu.SemaphoreType.DMA
    anywhere = pl.BlockSpec(memory_space=pltpu.HBM)
    vmem = pltpu.VMEM
    block = vmem((tiles, tokens, 128), BF16)
    edge = vmem((tiles, 128, 128), BF16)
    return pl.pallas_call(
        functools.partial(whole_kernel, *scales),
        in_specs=[anywhere] * 7,
        out_specs=[pl.BlockSpec(memory_space=pltpu.VMEM)] * 6,
        out_shape=[jax.ShapeDtypeStruct((tokens, channels), BF16)] * 4
        + [
            jax.ShapeDtypeStruct((layers, 2, XS, *slice_shape), F32),
            jax.ShapeDtypeStruct((tiles, 128), F32),
        ],
        scratch_shapes=[block] * 4
        + [vmem((channels // 16, 128), F32), vmem((tiles, 128), F32), vmem(starts.shape, jnp.int32)]
        + [edge] * 4
        + [vmem((tiles, 128, 384), BF16)] * 2
        + [block]
        + [vmem((5, 128, 128), BF16), vmem((4, 128, 128), F32)]
        + [vmem((128, 256), F32)] * 2
        + [
            vmem((2, XS, *slice_shape), F32), vmem((XS, *slice_shape), F32),
            vmem((XS, *slice_shape), F32), vmem((columns, *slice_shape), F32),
            vmem((tiles, 128), F32), vmem((1 + XS, tiles, 128), F32),
            vmem((columns, tiles, 128), F32),
        ]
        + [dma((4, tiles)), dma((3,))]
        + [dma((tiles,))] * 4
        + [dma, dma, dma((XS,)), dma((XS,)), dma((columns,)), dma((columns,))]
        + [dma, dma, dma((XS,)), dma((XS,)), dma((columns,)), dma((columns,))]
        + [dma((layers,)), dma((layers,)), dma((XS,)), dma((XS,)), dma((XS,)), dma((XS,))],
        compiler_params=pltpu.CompilerParams(
            collective_id=0, has_side_effects=True, vmem_limit_bytes=20 * 2**20
        ),
    )(*(pltpu.with_memory_space_constraint(a, pltpu.HBM) for a in (q, k, v, c, filters, skip, starts)))


def deliver_kernel(count, *refs):
    sem = refs[-1]
    copies = [
        pltpu.make_async_copy(refs[n], refs[count + n], sem.at[n]) for n in range(count)
    ]
    for copy in copies:
        copy.start()
    for copy in copies:
        copy.wait()


def deliver(*arrays):
    return pl.pallas_call(
        functools.partial(deliver_kernel, len(arrays)),
        in_specs=[pl.BlockSpec(memory_space=pltpu.VMEM)] * len(arrays),
        out_specs=[pl.BlockSpec(memory_space=pl.ANY)] * len(arrays),
        out_shape=[jax.ShapeDtypeStruct(a.shape, a.dtype) for a in arrays],
        scratch_shapes=[pltpu.SemaphoreType.DMA((len(arrays),))],
        compiler_params=pltpu.CompilerParams(vmem_limit_bytes=20 * 2**20),
    )(*arrays)


def body(q, k, v, c, filters, skip, contig_start):
    tokens, channels = q.shape
    group_total, taps = filters.shape
    count, layers = lax.axis_size("ctx"), lax.axis_size("tp")
    token_count = tokens * count
    per_group = channels * layers // group_total
    scales = 1.0 / math.sqrt(token_count * per_group), 1.0 / math.sqrt(token_count)
    results = whole(
        count // (2 * XS), layers, scales, q, k, v, c, filters,
        skip.reshape(channels // 128, 128), contig_start.reshape(token_count // 128, 128),
    )
    o, gq, gk, gv, total, bias_total = deliver(*results)
    return o, gq, gk, gv, total.reshape(group_total, taps), bias_total.reshape(channels)


def solution(mesh):
    return jax.shard_map(
        body,
        mesh=mesh,
        in_specs=(P("ctx", "tp"),) * 4 + (P(), P("tp"), P()),
        out_specs=(P("ctx", "tp"),) * 4 + (P(), P("tp")),
        check_vma=False,
    )
```

time: 612 us -> 44.4 us (0.07)
  waiting for transfers between devices: 266 us -> 0 us
  blocking collectives: 129 us -> 0 us
  local copies, waits for them, and re-layouts: 81.4 us -> 0 us
  starting transfers between devices: 52.1 us -> 0 us
  Pallas kernels: 0 us -> 43.6 us
  other arithmetic: 36.6 us -> 0 us
  matrix products: 16.5 us -> 0 us
  between operations: 14.4 us -> 0.64 us
  loops' own time: 12.7 us -> 0 us
    psum x1 -> x0, waiting for transfers between devices: 152 us -> none  [body(): filter_sum = lax.psum(filter_part, ('ctx', 'tp'))]
    psum x1 -> x0, blocking collectives: 129 us -> none  [body(): bias_sum = lax.psum(bias_part, 'ctx')]
    all_to_all x8 -> x0, waiting for transfers between devices: 115 us -> none  [the longest x1 16.7 us: body(): lax.all_to_all(queries, 'ctx', split_axis=1, concat_axis=0, tiled=True)]
    all_to_all x8 -> x0, starting transfers between devices: 52 us -> none  [the longest x1 11.7 us: body(): lax.all_to_all(key_branch, 'ctx', split_axis=1, concat_axis=0, tiled=True)]
    pallas_call x0 -> x2, Pallas kernels: none -> 43.6 us  [the longest x1 42.1 us: whole(): pl.pallas_call(functools.partial(whole_kernel, *scales), in_specs=[anywhe...]
    dynamic_slice x65 -> x0, local copies, waits for them, and re-layouts: 24.2 us -> none  [the longest x16 12.8 us: one_slab(): lax.dynamic_slice_in_dim(grad_pad, first_row + slab_rows, filter_size - 1...]
    dot_general x48 -> x0, matrix products: 16.5 us -> none  [the longest x16 5.89 us: hyena_pass(): jnp.einsum('btgc,bsgc->bgts', grads_ext[:block_count], windows, preferred...]
    reduce_sum x34 -> x0, other arithmetic: 14.7 us -> none  [the longest x16 14.1 us: hyena_pass(): jnp.sum(signal_grad.astype(jnp.float32) * gated_signal.astype(jnp.float32...]
  transfers between devices with their start and end apart: 9 -> 0, of which waited for: 8 -> 0; matrix products, arithmetic and copies ran while one was open for 2% -> 0% of each run, Pallas kernels for 0% -> 0%
where the time goes in v2:
time: 44.4 us; the launch traced here: 44.2 us
  Pallas kernels  43.6 us (98%)
  between operations  0.64 us (1%)
    pallas_call x1, Pallas kernels, whole(): pl.pallas_call(functools.partial(whole_kernel, *scales), in_specs=[anywhe...  42.1 us
    pallas_call x1, Pallas kernels, deliver(): pl.pallas_call(functools.partial(deliver_kernel, len(arrays)), in_specs=[...  1.45 us

profile of v2, /device:TPU:1, one launch (start us, length us, event | category | flops | bytes accessed | tf_op | source)
XLA Modules:
  0.0 44.2 jit_solution(4547612775546777095)
XLA Ops:
  0.6 42.1 %shard_map.118 = (bf16[256,1024]{1,0:T(8,128)(2,1)S(1)}, bf16[256,1024]{1,0:T(8,128)(2,1)S(1)}, bf16[256,1024]{1,0:T(8,128)(2,1)S(1)}, bf16[256,1024]{1,0:T(8,12...) custom-call(bf16[256,1024]{1,0:T(8,128)(2,1)} %q_hbm.1, bf16[256,1024]{1,0:T(8,128)(2,1)} %k_hbm.1, ...), custom_call_target="tpu_custom_call" | custom-call | tf_op jit(solution)/shard_map/pallas_call | solution.py:317
  42.8 1.5 %shard_map.119 = (bf16[256,1024]{1,0:T(8,128)(2,1)}, bf16[256,1024]{1,0:T(8,128)(2,1)}, bf16[256,1024]{1,0:T(8,128)(2,1)}, bf16[256,1024]{1,0:T(8,128)(2,1)}, f3...) custom-call(bf16[256,1024]{1,0:T(8,128)(2,1)S(1)} %get-tuple-element.18.refs_0_, ...), custom_call_target="tpu_custom_call" | custom-call | tf_op jit(solution)/shard_map/pallas_call | solution.py:362

commit v3 on v2

--- a/solution.py
+++ b/solution.py
@@ -32,10 +32,10 @@
     q_ref, k_ref, v_ref, c_ref, taps_ref, skip_ref, starts_ref,
     u_edge, g_edge, u_halo, g_halo, u_turned, g_turned, u_flip,
     pair_ref, lag_ref, ct_ref, bt_ref,
-    part, half_in, x_in, y_in, bias_part, bias_x, bias_y,
+    acc, part, half_in, x_in, y_in, bias_part, bias_x, bias_y,
     in_sem, misc_sem, us, ur, gs, gr,
     c_s, c_r, x_s, x_r, y_s, y_r, bc_s, bc_r, bx_s, bx_r, by_s, by_r,
-    z_s, z_r, gx_s, gx_r, gc_s, gc_r,
+    z_s, z_r, gc_s, gc_r,
 ):
     shard, z = lax.axis_index("ctx"), lax.axis_index("tp")
     count, layers = lax.axis_size("ctx"), lax.axis_size("tp")
@@ -82,8 +82,11 @@
     friends = [left, right, other] + [along_x(step)[1] for step in range(1, XS)]
     friends += [along_y(step)[1] for step in range(1, columns)]
     friends += [along_z(step)[1] for step in range(1, layers)]
-    for friend in friends:
-        pl.semaphore_signal(barrier, inc=1, device_id=friend, device_id_type=MESH)
+    def greet(some):
+        for friend in some:
+            pl.semaphore_signal(barrier, inc=1, device_id=friend, device_id_type=MESH)
+
+    greet(friends[:2])
 
     @pl.loop(0, tiles)
     def _(i):
@@ -92,6 +95,7 @@
 
     for copy in small:
         copy.start()
+    greet(friends[2:])
 
     s, t = iotas()
     flip = (s + t == 127).astype(F32).astype(BF16)
@@ -152,17 +156,16 @@
     start = [jnp.broadcast_to(row, (128, 128)) for row in rows]
     lower = (s <= t).astype(F32)
     turned = 127 - s
-    upper = (turned <= t).astype(F32)
+    above = turned <= t
     for b in range(3):
         pair_ref[2 * b] = ((1.0 - lower) * (s + 128 * (b - 1) >= start[b]).astype(F32)).astype(BF16)
         if b < 2:
             pair_ref[2 * b + 1] = (lower * (s + 128 * b >= start[b]).astype(F32)).astype(BF16)
-            lag_ref[2 * b] = upper * (turned + 128 * b >= start[b]).astype(F32)
-            lag_ref[2 * b + 1] = (1.0 - upper) * (turned + 128 * b >= start[b + 1]).astype(F32)
+            limit = jnp.where(above, start[b], start[b + 1])
+            lag_ref[b] = (turned + 128 * b >= limit).astype(F32)
 
     owner = lax.shift_right_logical(t, 4)
     none = jnp.zeros((128, 128), BF16)
-    above = turned <= t
 
     def fold(lags):
         lags = pltpu.roll(lags, 1, 1, stride=1, stride_axis=0)
@@ -171,22 +174,19 @@
     def part_rows(i):
         return part.at[i // XS, lax.rem(i, XS)]
 
+    def lags(i, n, b):
+        mine = jnp.where(owner == n, u_flip[i, 128 * b : 128 * b + 128], none)
+        products = dot(mine, g_turned[i, :, 128 * b : 128 * b + 256])
+        return jnp.where(above, products[:, :128], products[:, 128:]) * lag_ref[b]
+
     def own_lags(i):
-        mine_part = part_rows(i)
         for n in range(8):
-            mine = owner == n
-            first = dot(jnp.where(mine, u_flip[i, 0:128], none), g_turned[i, :, 0:256])
-            second = dot(jnp.where(mine, u_flip[i, 128:256], none), g_turned[i, :, 128:256])
-            lags = jnp.where(above, first[:, :128] , first[:, 128:]) * (lag_ref[0] + lag_ref[1])
-            mine_part[n : n + 1, :] = fold(lags + second * lag_ref[2])
+            acc[i, n] = lags(i, n, 0)
 
     def halo_lags(i):
-        mine_part = part_rows(i)
-        g_turned[i, :, 256:384] = g_halo[i].T
         for n in range(8):
-            mine = owner == n
-            far = dot(jnp.where(mine, u_flip[i, 128:256], none), g_turned[i, :, 256:384])
-            mine_part[n : n + 1, :] += fold(far * lag_ref[3])
+            both = pltpu.roll(acc[i, n] + lags(i, n, 1), 1, 1, stride=1, stride_axis=0)
+            part[i // XS, lax.rem(i, XS), n : n + 1] = jnp.sum(both, axis=0, keepdims=True)
 
     send(bias_part, bias_x.at[0], bc_s, bc_r, other)
 
@@ -200,10 +200,14 @@
         _, to = along_x(step)
         send(bias_x.at[1 + x], bias_x.at[1 + x], bx_s.at[step], bx_r.at[x], to)
 
-    @pl.loop(0, tiles, unroll=2)
-    def _(i):
-        g_copy(i).wait_recv()
-        halo_lags(i)
+    @pl.loop(0, tiles // 2)
+    def _(j):
+        for i in range(2):
+            g_copy(2 * j + i).wait_recv()
+        for i in range(2):
+            g_turned[2 * j + i, :, 256:384] = g_halo[2 * j + i].T
+        for i in range(2):
+            halo_lags(2 * j + i)
 
     send(part.at[1 - core], half_in, c_s, c_r, other)
 
@@ -254,7 +258,7 @@
         send(part.at[core, to_x], x_in.at[x], x_s.at[step], x_r.at[x], to)
     x_in[x] = part[core, x]
 
-    pl.loop(0, tiles // 2, unroll=2)(conv)
+    pl.loop(0, tiles // 2)(conv)
 
     for step in range(1, XS):
         source, to = along_x(step)
@@ -264,43 +268,44 @@
         _, to = along_y(step)
         send(y_in.at[y], y_in.at[y], y_s.at[step], y_r.at[y], to)
 
-    pl.loop(tiles // 2, tiles, unroll=2)(conv)
+    pl.loop(tiles // 2, tiles)(conv)
 
     for step in range(1, columns):
         source, to = along_y(step)
         remote(y_in.at[y], y_in.at[source], y_s.at[step], y_r.at[source], to).wait_recv()
     total[z, core, x] = jnp.sum(y_in[...], axis=0) * filter_scale
-    for step in range(1, layers):
-        _, to = along_z(step)
-        send(total.at[z, core, x], total.at[z, core, x], z_s.at[step], z_r.at[z], to)
+    own = total.at[z, core, x]
+    sheet = sorted(
+        ((a, b) for a in range(layers) for b in range(XS) if a or b),
+        key=lambda ab: -(min(ab[0], layers - ab[0]) + min(ab[1], XS - ab[1])),
+    )
+    for a, b in sheet:
+        to = device(y, lax.rem(x + b, XS), core, lax.rem(z + a, layers))
+        send(own, own, z_s.at[a, b], z_r.at[z, x], to)
 
     for step in range(1, columns):
         source, to = along_y(step)
         remote(bias_y.at[y], bias_y.at[source], by_s.at[step], by_r.at[source], to).wait_recv()
     bias_total[...] = jnp.sum(bias_y[...], axis=0) * bias_scale
 
-    for step in range(1, layers):
-        source, to = along_z(step)
-        remote(total.at[z, core, x], total.at[source, core, x], z_s.at[step], z_r.at[source], to).wait_recv()
-    block = total.at[:, core, x]
-    for step in range(1, XS):
-        _, to = along_x(step)
-        send(block, block, gx_s.at[step], gx_r.at[x], to)
-    send(block, block, gc_s.at[x], gc_r.at[x], other)
-    for step in range(1, XS):
-        source, to = along_x(step)
-        block = total.at[:, core, source]
-        remote(block, block, gx_s.at[step], gx_r.at[source], to).wait_recv()
-        send(block, block, gc_s.at[source], gc_r.at[source], other)
-
     @pl.loop(0, tiles)
     def _(i):
         u_copy(i).wait_send()
         g_copy(i).wait_send()
 
-    for source in range(XS):
-        block = total.at[:, 1 - core, source]
-        remote(block, block, gc_s.at[source], gc_r.at[source], other).wait_recv()
+    span = layers // 2
+    for chunk in range(2):
+        for a in range(chunk * span, chunk * span + span):
+            for b in range(XS):
+                @pl.when((a != z) | (b != x))
+                def _():
+                    there = total.at[a, core, b]
+                    remote(there, there, z_s.at[0, 0], z_r.at[a, b], other).wait_recv()
+        block = total.at[chunk * span : chunk * span + span, core]
+        send(block, block, gc_s.at[chunk], gc_r.at[chunk], other)
+    for chunk in range(2):
+        block = total.at[chunk * span : chunk * span + span, 1 - core]
+        remote(block, block, gc_s.at[chunk], gc_r.at[chunk], other).wait_recv()
     for descriptor in sent:
         descriptor.wait_send()
 
@@ -328,9 +333,10 @@
         + [edge] * 4
         + [vmem((tiles, 128, 384), BF16)] * 2
         + [block]
-        + [vmem((5, 128, 128), BF16), vmem((4, 128, 128), F32)]
+        + [vmem((5, 128, 128), BF16), vmem((2, 128, 128), F32)]
         + [vmem((128, 256), F32)] * 2
         + [
+            vmem((tiles, 8, 128, 128), F32),
             vmem((2, XS, *slice_shape), F32), vmem((XS, *slice_shape), F32),
             vmem((XS, *slice_shape), F32), vmem((columns, *slice_shape), F32),
             vmem((tiles, 128), F32), vmem((1 + XS, tiles, 128), F32),
@@ -340,9 +346,9 @@
         + [dma((tiles,))] * 4
         + [dma, dma, dma((XS,)), dma((XS,)), dma((columns,)), dma((columns,))]
         + [dma, dma, dma((XS,)), dma((XS,)), dma((columns,)), dma((columns,))]
-        + [dma((layers,)), dma((layers,)), dma((XS,)), dma((XS,)), dma((XS,)), dma((XS,))],
+        + [dma((layers, XS)), dma((layers, XS)), dma((2,)), dma((2,))],
         compiler_params=pltpu.CompilerParams(
-            collective_id=0, has_side_effects=True, vmem_limit_bytes=20 * 2**20
+            collective_id=0, has_side_effects=True, vmem_limit_bytes=24 * 2**20
         ),
     )(*(pltpu.with_memory_space_constraint(a, pltpu.HBM) for a in (q, k, v, c, filters, skip, starts)))
 

time: 44.4 us -> 41.9 us (0.944)
  Pallas kernels: 43.6 us -> 41 us
    pallas_call x1, Pallas kernels: 42.1 us -> 39.6 us  [whole(): pl.pallas_call(functools.partial(whole_kernel, *scales), in_specs=[anywhe...]
where the time goes in v3:
time: 41.9 us; the launch traced here: 41.7 us
  Pallas kernels  41 us (98%)
  between operations  0.64 us (2%)
    pallas_call x1, Pallas kernels, whole(): pl.pallas_call(functools.partial(whole_kernel, *scales), in_specs=[anywhe...  39.6 us
    pallas_call x1, Pallas kernels, deliver(): pl.pallas_call(functools.partial(deliver_kernel, len(arrays)), in_specs=[...  1.45 us

profile of v3, /device:TPU:1, one launch (start us, length us, event | category | flops | bytes accessed | tf_op | source)
XLA Modules:
  0.0 41.7 jit_solution(16790626272983138461)
XLA Ops:
  0.6 39.6 %shard_map.118 = (bf16[256,1024]{1,0:T(8,128)(2,1)S(1)}, bf16[256,1024]{1,0:T(8,128)(2,1)S(1)}, bf16[256,1024]{1,0:T(8,128)(2,1)S(1)}, bf16[256,1024]{1,0:T(8,12...) custom-call(bf16[256,1024]{1,0:T(8,128)(2,1)} %q_hbm.1, bf16[256,1024]{1,0:T(8,128)(2,1)} %k_hbm.1, ...), custom_call_target="tpu_custom_call" | custom-call | tf_op jit(solution)/shard_map/pallas_call | solution.py:322
  40.2 1.5 %shard_map.119 = (bf16[256,1024]{1,0:T(8,128)(2,1)}, bf16[256,1024]{1,0:T(8,128)(2,1)}, bf16[256,1024]{1,0:T(8,128)(2,1)}, bf16[256,1024]{1,0:T(8,128)(2,1)}, f3...) custom-call(bf16[256,1024]{1,0:T(8,128)(2,1)S(1)} %get-tuple-element.18.refs_0_, ...), custom_call_target="tpu_custom_call" | custom-call | tf_op jit(solution)/shard_map/pallas_call | solution.py:368

commit v4 on v3

--- a/solution.py
+++ b/solution.py
@@ -23,6 +23,14 @@
 
 def dot(a, b):
     return jnp.dot(a, b, preferred_element_type=F32)
+
+
+def near(size):
+    return sorted({1, 2, size - 2, size - 1} & set(range(1, size)))
+
+
+def beyond(size):
+    return [2, size - 2] if size > 5 else []
 
 
 def whole_kernel(
@@ -35,17 +43,20 @@
     acc, part, half_in, x_in, y_in, bias_part, bias_x, bias_y,
     in_sem, misc_sem, us, ur, gs, gr,
     c_s, c_r, x_s, x_r, y_s, y_r, bc_s, bc_r, bx_s, bx_r, by_s, by_r,
-    z_s, z_r, gc_s, gc_r,
+    z_s, z_r, gc_s, gc_r, ready_sem,
 ):
     shard, z = lax.axis_index("ctx"), lax.axis_index("tp")
     count, layers = lax.axis_size("ctx"), lax.axis_size("tp")
     columns = count // (2 * XS)
-    tiles = q_ref.shape[0]
+    tiles = q_ref.shape[1] // 128
     groups = part.shape[0] * part.shape[1] * part.shape[2]
     y, x, core = shard // (2 * XS), lax.rem(shard, 2 * XS) // 2, lax.rem(shard, 2)
 
     def device(to_y, to_x, to_core, to_z):
         return {"ctx": (to_y * XS + to_x) * 2 + to_core, "tp": to_z}
+
+    def far_first(size):
+        return sorted(range(1, size), key=lambda step: -min(step, size - step))
 
     def along_x(step):
         to = lax.rem(x + step, XS)
@@ -63,14 +74,18 @@
     right = {"ctx": lax.rem(shard + 1, count), "tp": z}
     left = {"ctx": lax.rem(shard + count - 1, count), "tp": z}
 
-    def inputs(i):
-        lanes = pl.ds(pl.multiple_of(i * 128, 128), 128)
-        return [
-            pltpu.make_async_copy(hbm.at[:, lanes], ref.at[i], in_sem.at[n, i])
-            for n, (hbm, ref) in enumerate(
-                ((q_hbm, q_ref), (k_hbm, k_ref), (v_hbm, v_ref), (c_hbm, c_ref))
-            )
+    def lanes_of(i):
+        return pl.ds(pl.multiple_of(i * 128, 128), 128)
+
+    low, high = pl.ds(0, 128), pl.ds(128, 128)
+    sources = ((q_hbm, q_ref), (c_hbm, c_ref), (k_hbm, k_ref), (v_hbm, v_ref))
+    edges, inner = (
+        [
+            pltpu.make_async_copy(hbm.at[rows], ref.at[rows], in_sem.at[base + n])
+            for n, ((hbm, ref), rows) in enumerate(zip(sources, order))
         ]
+        for base, order in ((0, (low, low, high, high)), (4, (high, high, low, low)))
+    )
 
     small = [
         pltpu.make_async_copy(starts_hbm, starts_ref, misc_sem.at[0]),
@@ -80,20 +95,17 @@
 
     barrier = pltpu.get_barrier_semaphore()
     friends = [left, right, other] + [along_x(step)[1] for step in range(1, XS)]
-    friends += [along_y(step)[1] for step in range(1, columns)]
-    friends += [along_z(step)[1] for step in range(1, layers)]
+    friends += [along_y(step)[1] for step in near(columns)]
+    friends += [along_z(step)[1] for step in near(layers)]
+    scouts = [along_y(step)[1] for step in beyond(columns)]
+    scouts += [along_z(step)[1] for step in beyond(layers)]
     def greet(some):
         for friend in some:
             pl.semaphore_signal(barrier, inc=1, device_id=friend, device_id_type=MESH)
 
     greet(friends[:2])
 
-    @pl.loop(0, tiles)
-    def _(i):
-        for copy in inputs(i):
-            copy.start()
-
-    for copy in small:
+    for copy in edges + inner + small:
         copy.start()
     greet(friends[2:])
 
@@ -101,15 +113,18 @@
     flip = (s + t == 127).astype(F32).astype(BF16)
 
     def gates(i):
-        q, k, v, c = (ref[i].astype(F32) for ref in (q_ref, k_ref, v_ref, c_ref))
+        lanes = lanes_of(i)
+        q, k, v, c = (ref[:, lanes].astype(F32) for ref in (q_ref, k_ref, v_ref, c_ref))
         return q, k, v, c, (k * v).astype(BF16), (c * q).astype(BF16)
 
+    for copy in edges:
+        copy.wait()
+
     @pl.loop(0, tiles)
     def _(i):
-        for copy in inputs(i):
-            copy.wait()
-        u_edge[i] = (k_ref[i, 128:256].astype(F32) * v_ref[i, 128:256].astype(F32)).astype(BF16)
-        g_edge[i] = (c_ref[i, 0:128].astype(F32) * q_ref[i, 0:128].astype(F32)).astype(BF16)
+        lanes = lanes_of(i)
+        g_edge[i] = (c_ref[low, lanes].astype(F32) * q_ref[low, lanes].astype(F32)).astype(BF16)
+        u_edge[i] = (k_ref[high, lanes].astype(F32) * v_ref[high, lanes].astype(F32)).astype(BF16)
 
     pl.semaphore_wait(barrier, len(friends))
     sent = []
@@ -138,6 +153,12 @@
     @pl.loop(0, tiles)
     def _(i):
         u_copy(i).start()
+
+    for scout in scouts:
+        pl.semaphore_signal(ready_sem, inc=1, device_id=scout, device_id_type=MESH)
+
+    for copy in inner:
+        copy.wait()
 
     @pl.loop(0, tiles, unroll=2)
     def _(i):
@@ -194,6 +215,8 @@
     def _(i):
         own_lags(i)
 
+    if scouts:
+        pl.semaphore_wait(ready_sem, len(scouts))
     remote(bias_part, bias_x.at[0], bc_s, bc_r, other).wait_recv()
     bias_x[1 + x] = bias_part[...] + bias_x[0]
     for step in range(1, XS):
@@ -244,7 +267,7 @@
             )
         skip = skip_ref[pl.ds(i, 1)]
         filtered = ct_ref[...].T + skip * u.astype(F32)
-        lanes = pl.ds(pl.multiple_of(i * 128, 128), 128)
+        lanes = lanes_of(i)
         o_ref[:, lanes] = (q * filtered).astype(BF16)
         gq_ref[:, lanes] = (c * filtered).astype(BF16)
         gated_grad = bt_ref[...].T + skip * g.astype(F32)
@@ -253,7 +276,7 @@
 
     remote(part.at[1 - core], half_in, c_s, c_r, other).wait_recv()
     part[core] += half_in[...]
-    for step in range(1, XS):
+    for step in far_first(XS):
         to_x, to = along_x(step)
         send(part.at[core, to_x], x_in.at[x], x_s.at[step], x_r.at[x], to)
     x_in[x] = part[core, x]
@@ -264,7 +287,7 @@
         source, to = along_x(step)
         remote(x_in.at[x], x_in.at[source], x_s.at[step], x_r.at[source], to).wait_recv()
     y_in[y] = x_in[0] + x_in[1] + x_in[2] + x_in[3]
-    for step in range(1, columns):
+    for step in far_first(columns):
         _, to = along_y(step)
         send(y_in.at[y], y_in.at[y], y_s.at[step], y_r.at[y], to)
 
@@ -293,6 +316,11 @@
         u_copy(i).wait_send()
         g_copy(i).wait_send()
 
+    sheet_sends = sent[-len(sheet) :]
+    for descriptor in sent[: -len(sheet)]:
+        descriptor.wait_send()
+    sent.clear()
+
     span = layers // 2
     for chunk in range(2):
         for a in range(chunk * span, chunk * span + span):
@@ -303,6 +331,8 @@
                     remote(there, there, z_s.at[0, 0], z_r.at[a, b], other).wait_recv()
         block = total.at[chunk * span : chunk * span + span, core]
         send(block, block, gc_s.at[chunk], gc_r.at[chunk], other)
+    for descriptor in sheet_sends:
+        descriptor.wait_send()
     for chunk in range(2):
         block = total.at[chunk * span : chunk * span + span, 1 - core]
         remote(block, block, gc_s.at[chunk], gc_r.at[chunk], other).wait_recv()
@@ -328,7 +358,7 @@
             jax.ShapeDtypeStruct((layers, 2, XS, *slice_shape), F32),
             jax.ShapeDtypeStruct((tiles, 128), F32),
         ],
-        scratch_shapes=[block] * 4
+        scratch_shapes=[vmem((tokens, channels), BF16)] * 4
         + [vmem((channels // 16, 128), F32), vmem((tiles, 128), F32), vmem(starts.shape, jnp.int32)]
         + [edge] * 4
         + [vmem((tiles, 128, 384), BF16)] * 2
@@ -342,11 +372,11 @@
             vmem((tiles, 128), F32), vmem((1 + XS, tiles, 128), F32),
             vmem((columns, tiles, 128), F32),
         ]
-        + [dma((4, tiles)), dma((3,))]
+        + [dma((8,)), dma((3,))]
         + [dma((tiles,))] * 4
         + [dma, dma, dma((XS,)), dma((XS,)), dma((columns,)), dma((columns,))]
         + [dma, dma, dma((XS,)), dma((XS,)), dma((columns,)), dma((columns,))]
-        + [dma((layers, XS)), dma((layers, XS)), dma((2,)), dma((2,))],
+        + [dma((layers, XS)), dma((layers, XS)), dma((2,)), dma((2,)), pltpu.SemaphoreType.REGULAR],
         compiler_params=pltpu.CompilerParams(
             collective_id=0, has_side_effects=True, vmem_limit_bytes=24 * 2**20
         ),

time: 41.9 us -> 40.4 us (0.964)
  Pallas kernels: 41 us -> 39.6 us
    pallas_call x1, Pallas kernels: 39.6 us -> 38.1 us  [whole(): pl.pallas_call(functools.partial(whole_kernel, *scales), in_specs=[anywhe...]
where the time goes in v4:
time: 40.4 us; the launch traced here: 40.2 us
  Pallas kernels  39.6 us (98%)
  between operations  0.64 us (2%)
    pallas_call x1, Pallas kernels, whole(): pl.pallas_call(functools.partial(whole_kernel, *scales), in_specs=[anywhe...  38.1 us
    pallas_call x1, Pallas kernels, deliver(): pl.pallas_call(functools.partial(deliver_kernel, len(arrays)), in_specs=[...  1.45 us

profile of v4, /device:TPU:1, one launch (start us, length us, event | category | flops | bytes accessed | tf_op | source)
XLA Modules:
  0.0 40.2 jit_solution(2207888335951314705)
XLA Ops:
  0.6 38.1 %shard_map.118 = (bf16[256,1024]{1,0:T(8,128)(2,1)S(1)}, bf16[256,1024]{1,0:T(8,128)(2,1)S(1)}, bf16[256,1024]{1,0:T(8,128)(2,1)S(1)}, bf16[256,1024]{1,0:T(8,12...) custom-call(bf16[256,1024]{1,0:T(8,128)(2,1)} %q_hbm.1, bf16[256,1024]{1,0:T(8,128)(2,1)} %k_hbm.1, ...), custom_call_target="tpu_custom_call" | custom-call | tf_op jit(solution)/shard_map/pallas_call | solution.py:352
  38.8 1.5 %shard_map.119 = (bf16[256,1024]{1,0:T(8,128)(2,1)}, bf16[256,1024]{1,0:T(8,128)(2,1)}, bf16[256,1024]{1,0:T(8,128)(2,1)}, bf16[256,1024]{1,0:T(8,128)(2,1)}, f3...) custom-call(bf16[256,1024]{1,0:T(8,128)(2,1)S(1)} %get-tuple-element.18.refs_0_, ...), custom_call_target="tpu_custom_call" | custom-call | tf_op jit(solution)/shard_map/pallas_call | solution.py:398
